TPU v7x, 512 devices: a whole 4x4x16 slice. The times are simulated.
512 devices in a mesh: sub: 64 (over x, z), grp: 8 (over y, core).
Axes of the slice: x: 4, y: 4, z: 16, core: 2. Of those that a mesh axis runs over, the one named last changes fastest.
Arguments:
- rhs_jump: float32 [64, 8, 256, 256], P('sub', 'grp'), may hold values from -6 to 6
- incision: int32 [64, 8, 256], P('sub', 'grp'), may hold values 0 or 1
- precond: float32 [64, 8, 256], P('sub', 'grp'), may hold values from 0.5 to 2
- left_rows: int32 [64, 8, 256], P('sub', 'grp'), may hold values from 0 to 1151, as said below
- right_rows: int32 [64, 8, 256], P('sub', 'grp'), may hold values from 0 to 1151, as said below
- diag_inv: float32 [64, 8, 3, 384, 384], P('sub', 'grp'), as said below
- coupling: float32 [64, 8, 2, 384, 384], P('sub', 'grp'), may hold values from -0.09185587 to 0.09185587
- coarse_basis: float32 [64, 8, 3, 384, 128], P('sub', 'grp'), may hold values from -0.25 to 0.25
- coarse_inv: float32 [64, 128, 128], P('sub'), as said below
Outputs:
- multipliers: float32 [64, 8, 256, 256], P('sub', 'grp')
- residual: float32 [64, 8, 256, 256], P('sub', 'grp')
Inputs may be any that keep to these rules, and one draw needn't show every extreme that they name: `left_rows`: for each subdomain, its 256 left rows and 256 right rows are 512 distinct interior rows. `right_rows`: see left_rows. `diag_inv`: every block is invertible. `coarse_inv`: every block is symmetric positive definite.
All inputs are finite; a program needn't handle non-finite values. No bound on the sum of `incision` on one device may be relied on, other than what follows from the above.
Results may differ from a plain program's by a relative error of at most 0.0003.
Values sent between devices are 32-bit elements; how exact they have to be, the bound alone decides.
No kernel may reach another device: no remote copies, remote signals or barrier semaphores. Data moves between devices by JAX's collectives and lax.ppermute only.
A program may use at most 64 MiB of HBM per device.

v0:
```python
import jax
import jax.numpy as jnp
from jax import lax
from jax.sharding import PartitionSpec as P

ITERS = 3
HIGH = lax.Precision.HIGHEST


def passed_along(shard, axis, by):
    peers = lax.axis_size(axis)
    return lax.ppermute(shard, axis, [(i, (i + by) % peers) for i in range(peers)])


def norm_total(value):
    return lax.psum(value, ("sub", "grp"))


def local(
    rhs_jump, incision, precond, left_rows, right_rows, diag_inv, coupling, coarse_basis, coarse_inv
):
    load_rhs = rhs_jump[0, 0]
    cut = incision[0, 0].astype(jnp.float32)[:, None]
    scaling = precond[0, 0][:, None]
    lrow = left_rows[0, 0]
    rrow = right_rows[0, 0]
    dinv = diag_inv[0, 0]
    coup = coupling[0, 0]
    nblk, blk = (dinv.shape[0], dinv.shape[1])
    order = nblk * blk
    basis = coarse_basis[0, 0].reshape(order, -1)
    cinv = coarse_inv[0]
    width = load_rhs.shape[1]
    start = load_rhs[None]
    scales = scaling[None]
    cuts = cut[None]

    def local_dot(first, second):
        return jnp.sum(first[-1] * second[-1], axis=0)

    multipliers = jnp.zeros_like(start)
    residual = cuts * start
    zvec = scales * residual
    direc = zvec
    rz_now = norm_total(local_dot(residual, zvec))
    for step in range(ITERS):
        apply_own = direc[0]
        apply_left = passed_along(apply_own, "sub", 1)
        zeros = jnp.zeros((order, width), jnp.float32)
        interior_load = zeros.at[rrow].add(apply_own).at[lrow].add(-apply_left)
        primal = jnp.einsum("np,nr->pr", basis, interior_load, precision=HIGH)
        summed = lax.psum(primal, "grp")
        pieces = interior_load.reshape(nblk, blk, width)
        forward = []
        for block in range(nblk):
            rhs_now = pieces[block]
            if block > 0:
                rhs_now = rhs_now - jnp.dot(coup[block - 1], forward[-1], precision=HIGH)
            forward.append(jnp.dot(dinv[block], rhs_now, precision=HIGH))
        backward = [None] * nblk
        for block in range(nblk - 1, -1, -1):
            rhs_now = forward[block]
            if block < nblk - 1:
                rhs_now = rhs_now - jnp.dot(coup[block].T, backward[block + 1], precision=HIGH)
            backward[block] = jnp.dot(dinv[block].T, rhs_now, precision=HIGH)
        solved = jnp.concatenate(backward, axis=0)
        coarse = jnp.dot(cinv, summed, precision=HIGH)
        disp = solved + jnp.dot(basis, coarse, precision=HIGH)
        yleft = jnp.take(disp, lrow, axis=0)
        yright = jnp.take(disp, rrow, axis=0)
        nextone = passed_along(yleft, "sub", -1)
        image = (cut * (yright - nextone))[None]
        alpha = rz_now / lax.psum(local_dot(direc, image), ("sub", "grp"))
        multipliers = multipliers + alpha * direc
        residual = residual - alpha * image
        if step + 1 < ITERS:
            zvec = scales * residual
            rz_new = norm_total(local_dot(residual, zvec))
            direc = zvec + rz_new / rz_now * direc
            rz_now = rz_new
    return (multipliers[-1][None, None], residual[-1][None, None])


def solution(mesh):
    placed = (
        P("sub", "grp", None, None),
        P("sub", "grp", None),
        P("sub", "grp", None),
        P("sub", "grp", None),
        P("sub", "grp", None),
        P("sub", "grp", None, None, None),
        P("sub", "grp", None, None, None),
        P("sub", "grp", None, None, None),
        P("sub", None, None),
    )
    return jax.shard_map(
        local,
        mesh=mesh,
        in_specs=placed,
        out_specs=(P("sub", "grp", None, None), P("sub", "grp", None, None)),
        check_vma=False,
    )
```

profile of v0, /device:TPU:1, one launch (start us, length us, event | category | flops | bytes accessed | tf_op | source)
XLA Modules:
  0.0 924.1 jit_solution(12377833747426889409)
XLA Ops:
  9.1 4.4 collective-permute-start
  16.2 3.6 scatter_custom_fusion
  20.4 8.8 collective-permute-done
  29.9 4.7 scatter_custom_fusion.1
  34.7 2.5 fusion.46
  46.2 2.7 convolution_bitcast_fusion.14
  49.2 2.7 convolution_bitcast_fusion.9
  51.8 67.6 %all-reduce.5.cloned.1.call-done = f32[128,256]{0,1:T(8,128)} async-done(((f32[128,256]{0,1:T(8,128)}), f32[128,256]{0,1:T(8,128)}) %all-reduce.5.cloned.1.call-update) | async-done | bytes 131088 | tf_op jit(solution)/shard_map/psum | solution.py:52
  120.6 3.3 fusion.2
  123.9 2.7 copy.17
  126.6 2.9 gather_fusion.1
  131.3 7.0 collective-permute-start.1
  139.7 2.9 gather_fusion
  144.5 106.5 %all-reduce = (f32[256]{0:T(256)}, f32[256]{0:T(256)}) all-reduce(f32[256]{0:T(256)} %get-tuple-element.4, f32[256]{0:T(256)S(1)} %get-tuple-element.3), channel_id=1, replica_groups=mesh['sub'=64,'grp'=8] {'sub','grp'}, use_global_device_ids=true, to_apply=%region_1.0 | all-reduce | flops 512 | bytes 4096 | tf_op jit(solution)/shard_map/psum | solution.py:16
  251.7 2.6 fusion.87
  254.2 98.8 %psum.66 = f32[256]{0:T(256)S(1)} all-reduce(f32[256]{0:T(256)} %get-tuple-element.9), channel_id=1, replica_groups=mesh['sub'=64,'grp'=8] {'sub','grp'}, use_global_device_ids=true, to_apply=%region_8.10 | all-reduce | flops 256 | bytes 2048 | tf_op jit(solution)/shard_map/psum | solution.py:16
  353.7 1.9 multiply_add_fusion.1
  355.5 3.7 collective-permute-start.2
  359.2 3.4 scatter_custom_fusion.2
  362.6 5.6 collective-permute-done.2
  368.3 4.9 scatter_custom_fusion.3
  373.1 3.3 fusion.43
  376.4 2.7 convolution_bitcast_fusion.13
  379.1 1.9 convolution_bitcast_fusion.8
  390.2 2.6 convolution_bitcast_fusion.6
  392.8 62.3 %all-reduce.7.cloned.1.call-done = f32[128,256]{0,1:T(8,128)} async-done(((f32[128,256]{0,1:T(8,128)}), f32[128,256]{0,1:T(8,128)}) %all-reduce.7.cloned.1.call-update) | async-done | bytes 131088 | tf_op jit(solution)/shard_map/psum | solution.py:52
  456.4 3.4 fusion.1
  459.7 2.6 copy.19
  462.4 3.0 gather_fusion.3
  467.2 7.0 collective-permute-start.3
  474.2 3.1 gather_fusion.2
  479.6 107.2 %psum.68 = f32[256]{0:T(256)} all-reduce(f32[256]{0:T(256)} %multiply_reduce_fusion.1), channel_id=1, replica_groups=mesh['sub'=64,'grp'=8] {'sub','grp'}, use_global_device_ids=true, to_apply=%region_13.15 | all-reduce | flops 256 | bytes 2048 | tf_op jit(solution)/shard_map/psum | solution.py:73
  588.0 2.6 fusion.88
  590.6 98.5 %psum.69 = f32[256]{0:T(256)} all-reduce(f32[256]{0:T(256)} %get-tuple-element.7), channel_id=1, replica_groups=mesh['sub'=64,'grp'=8] {'sub','grp'}, use_global_device_ids=true, to_apply=%region_15.17 | all-reduce | flops 256 | bytes 2048 | tf_op jit(solution)/shard_map/psum | solution.py:16
  691.6 3.7 collective-permute-start.4
  695.3 3.4 scatter_custom_fusion.4
  698.7 5.7 collective-permute-done.4
  704.3 4.7 scatter_custom_fusion.5
  709.0 3.3 fusion.40
  712.3 2.7 convolution_bitcast_fusion.12
  715.0 1.9 convolution_bitcast_fusion.5
  725.9 3.0 convolution_bitcast_fusion.3
  728.8 62.6 %all-reduce.9.cloned.1.call-done = f32[128,256]{0,1:T(8,128)} async-done(((f32[128,256]{0,1:T(8,128)}), f32[128,256]{0,1:T(8,128)}) %all-reduce.9.cloned.1.call-update) | async-done | bytes 131088 | tf_op jit(solution)/shard_map/psum | solution.py:52
  792.6 2.2 fusion
  796.5 7.1 collective-permute-start.5
  804.7 2.2 collective-permute-done.5
  808.0 107.2 %psum.71 = f32[256]{0:T(256)S(1)} all-reduce(f32[256]{0:T(256)S(1)} %multiply_reduce_fusion), channel_id=1, replica_groups=mesh['sub'=64,'grp'=8] {'sub','grp'}, use_global_device_ids=true, to_apply=%region_20.22 | all-reduce | flops 256 | bytes 2048 | tf_op jit(solution)/shard_map/psum | solution.py:73
  915.3 2.0 subtract_bitcast_fusion
  (126 shorter events, 54.6 us)
Async XLA Ops:
  7.2 39.0 %copy-start = (f32[1,1,3,384,128]{4,3,2,1,0:T(8,128)S(1)}, f32[1,1,3,384,128]{4,3,2,1,0:T(8,128)}, u32[]{:S(2)}) copy-start(f32[1,1,3,384,128]{4,3,2,1,0:T(8,128)} %param.18) | copy-start | bytes 1769476
  7.2 12.7 %copy-start.31 = (s32[1,1,256]{2,1,0:T(1,128)S(1)}, s32[1,1,256]{2,1,0:T(1,128)}, u32[]{:S(2)}) copy-start(s32[1,1,256]{2,1,0:T(1,128)} %param.15) | copy-start | bytes 3076
  7.2 112.2 %all-reduce.5.cloned.1.call-start = ((), (), s32[]{:S(2)}) async-start(), calls=%async_computation | async-start | bytes 262144 | tf_op jit(solution)/shard_map/psum | solution.py:52
  9.1 20.1 %collective-permute-start = (f32[256,256]{1,0:T(8,128)S(1)}, f32[256,256]{1,0:T(8,128)S(1)}, u32[]{:S(2)}, u32[]{:S(2)}) collective-permute-start(f32[256,256]{1,0:T(8,128)S(1)} %fusion.98), channel_id=1, source_target_pairs={{0,8},{8,16},{16,24},{24,32},{32,40},{40,48},{48,56},{56,64},{64,7... | collective-permute-start | bytes 786440 | tf_op jit(solution)/shard_map/ppermute | solution.py:12
  14.1 20.5 %copy-start.32 = (s32[256,1]{0,1:T(1,128)}, s32[256,1]{0,1:T(1,128)S(1)}, u32[]{:S(2)}) copy-start(s32[256,1]{0,1:T(1,128)S(1)} %compare_select_fusion) | copy-start | bytes 3076
  15.5 114.1 %copy-start.29 = (pred[256]{0:T(512)(128)(4,1)}, pred[256]{0:T(512)(128)(4,1)S(1)}, u32[]{:S(2)}) copy-start(pred[256]{0:T(512)(128)(4,1)S(1)} %compare_and_fusion) | copy-start | bytes 772
  16.2 13.0 %copy-start.33 = (s32[256,1]{0,1:T(1,128)}, s32[256,1]{0,1:T(1,128)S(1)}, u32[]{:S(2)}) copy-start(s32[256,1]{0,1:T(1,128)S(1)} %compare_select_fusion.1) | copy-start | bytes 3076
  16.2 110.4 %copy-start.22 = (s32[1024]{0:T(1024)}, s32[1024]{0:T(1024)S(1)}, u32[]{:S(2)}) copy-start(s32[1024]{0:T(1024)S(1)} %pad_clamp_fusion) | copy-start | bytes 12292
  16.2 18.4 %copy-start.1 = (f32[1,1,3,384,384]{4,3,2,1,0:T(8,128)S(1)}, f32[1,1,3,384,384]{4,3,2,1,0:T(8,128)}, u32[]{:S(2)}) copy-start(f32[1,1,3,384,384]{4,3,2,1,0:T(8,128)} %param.16) | copy-start | bytes 5308420
  29.2 0.7 copy-start.20
  29.9 7.3 copy-start.2
  34.6 3.4 copy-start.7
  42.7 1.8 copy-start.9
  44.5 1.7 copy-start.10
  48.9 406.3 %all-reduce.7.cloned.1.call-start = ((), (), s32[]{:S(2)}) async-start(), calls=%async_computation.1 | async-start | bytes 262144 | tf_op jit(solution)/shard_map/psum | solution.py:52
  131.3 11.3 %collective-permute-start.1 = (f32[256,256]{1,0:T(8,128)}, f32[256,256]{1,0:T(8,128)}, u32[]{:S(2)}, u32[]{:S(2)}) collective-permute-start(f32[256,256]{1,0:T(8,128)} %broadcast_select_fusion.2), channel_id=1, source_target_pairs={{0,504},{8,0},{16,8},{24,16},{32,24},{40,32},{48,40},{56,48},{64,5... | collective-permute-start | bytes 786440 | tf_op jit(solution)/shard_map/ppermute | solution.py:12
  139.0 3.6 copy-start.23
  139.7 3.0 copy-start.21
  251.7 2.6 copy-start.25
  355.5 12.7 %collective-permute-start.2 = (f32[256,256]{1,0:T(8,128)}, f32[256,256]{1,0:T(8,128)}, u32[]{:S(2)}, u32[]{:S(2)}) collective-permute-start(f32[256,256]{1,0:T(8,128)} %multiply_add_fusion.1), channel_id=1, source_target_pairs={{0,8},{8,16},{16,24},{24,32},{32,40},{40,48},{48,56},{56,64},{64,7... | collective-permute-start | bytes 786440 | tf_op jit(solution)/shard_map/ppermute | solution.py:12
  373.1 3.3 copy-start.5
  379.1 1.9 copy-start.6
  385.7 1.8 copy-start.11
  385.7 2.6 copy-start.16
  387.5 0.7 copy-start.14
  390.0 401.5 %all-reduce.9.cloned.1.call-start = ((), (), s32[]{:S(2)}) async-start(), calls=%async_computation.2 | async-start | bytes 262144 | tf_op jit(solution)/shard_map/psum | solution.py:52
  467.2 10.6 %collective-permute-start.3 = (f32[256,256]{1,0:T(8,128)}, f32[256,256]{1,0:T(8,128)}, u32[]{:S(2)}, u32[]{:S(2)}) collective-permute-start(f32[256,256]{1,0:T(8,128)} %broadcast_select_fusion.1), channel_id=1, source_target_pairs={{0,504},{8,0},{16,8},{24,16},{32,24},{40,32},{48,40},{56,48},{64,5... | collective-permute-start | bytes 786440 | tf_op jit(solution)/shard_map/ppermute | solution.py:12
  587.4 0.6 copy-start.27
  691.6 12.7 %collective-permute-start.4 = (f32[256,256]{1,0:T(8,128)}, f32[256,256]{1,0:T(8,128)}, u32[]{:S(2)}, u32[]{:S(2)}) collective-permute-start(f32[256,256]{1,0:T(8,128)} %multiply_add_fusion), channel_id=1, source_target_pairs={{0,8},{8,16},{16,24},{24,32},{32,40},{40,48},{48,56},{56,64},{64,7... | collective-permute-start | bytes 786440 | tf_op jit(solution)/shard_map/ppermute | solution.py:12
  709.0 3.3 copy-start.3
  715.0 1.9 copy-start.4
  721.5 1.8 copy-start.12
  721.6 2.6 copy-start.17
  723.4 0.7 copy-start.15
  725.8 65.6 %copy-start.19 = (f32[1,128,128]{2,1,0:T(8,128)S(1)}, f32[1,128,128]{2,1,0:T(8,128)}, u32[]{:S(2)}) copy-start(f32[1,128,128]{2,1,0:T(8,128)} %param.19) | copy-start | bytes 196612
  725.8 66.8 %copy-start.13 = (f32[256,384]{1,0:T(8,128)S(1)}, f32[256,384]{1,0:T(8,128)}, u32[]{:S(2)}) copy-start(f32[256,384]{1,0:T(8,128)} %copy-done.12) | copy-start | bytes 1179652
  795.2 1.1 copy-start.30
  796.4 118.8 %copy-start.24 = (f32[256]{0:T(256)S(1)}, f32[256]{0:T(256)}, u32[]{:S(2)}) copy-start(f32[256]{0:T(256)} %psum.69) | copy-start | bytes 3076
  796.4 118.8 %copy-start.8 = (f32[1,1,256,256]{3,2,1,0:T(8,128)S(1)}, f32[1,1,256,256]{3,2,1,0:T(8,128)}, u32[]{:S(2)}) copy-start(f32[1,1,256,256]{3,2,1,0:T(8,128)} %param.11) | copy-start | bytes 786436
  796.5 118.8 %copy-start.18 = (f32[256,256]{1,0:T(8,128)S(1)}, f32[256,256]{1,0:T(8,128)}, u32[]{:S(2)}) copy-start(f32[256,256]{1,0:T(8,128)} %get-tuple-element.8) | copy-start | bytes 786436
  796.5 118.8 %copy-start.26 = (f32[256]{0:T(256)S(1)}, f32[256]{0:T(256)}, u32[]{:S(2)}) copy-start(f32[256]{0:T(256)} %copy-done.25) | copy-start | bytes 3076
  796.5 118.8 %copy-start.28 = (f32[256]{0:T(256)S(1)}, f32[256]{0:T(256)}, u32[]{:S(2)}) copy-start(f32[256]{0:T(256)} %copy-done.27) | copy-start | bytes 3076
  796.5 10.4 %collective-permute-start.5 = (f32[256,256]{1,0:T(8,128)S(1)}, f32[256,256]{1,0:T(8,128)S(1)}, u32[]{:S(2)}, u32[]{:S(2)}) collective-permute-start(f32[256,256]{1,0:T(8,128)S(1)} %broadcast_select_fusion), channel_id=1, source_target_pairs={{0,504},{8,0},{16,8},{24,16},{32,24},{40,32},{48,40},{56,48},{64,5... | collective-permute-start | bytes 786440 | tf_op jit(solution)/shard_map/ppermute | solution.py:12
Sparse Core Ops, SparseCore 0:
  49.0 70.3 all-reduce.4
  390.1 65.0 all-reduce.6
  726.0 65.3 all-reduce.8
where the time goes:
time: 929 us; the launch traced here: 924 us
  blocking collectives  518 us (56%)
  waiting for transfers between devices  215 us (23%)
  matrix products  66.8 us (7%)
  other arithmetic  53 us (6%)
  starting transfers between devices  33.3 us (4%)
  local copies, waits for them, and re-layouts  22.8 us (2%)
  between operations  14.6 us (2%)
    psum x3, blocking collectives, norm_total(): return lax.psum(value, ('sub', 'grp'))  304 us
    psum x2, blocking collectives, local(): alpha = rz_now / lax.psum(local_dot(direc, image), ('sub', 'grp'))  214 us
    psum x3, waiting for transfers between devices, local(): summed = lax.psum(primal, 'grp')  192 us
    ppermute x6, starting transfers between devices, passed_along(): lax.ppermute(shard, axis, [(i, (i + by) % peers) for i in range(peers)])  32.8 us
    scatter-add x6, other arithmetic, local(): interior_load = zeros.at[rrow].add(apply_own).at[lrow].add(-apply_left)  24.6 us
    ppermute x6, waiting for transfers between devices, passed_along(): lax.ppermute(shard, axis, [(i, (i + by) % peers) for i in range(peers)])  22.8 us
  transfers between devices with their start and end apart: 9, of which 8 were waited for; matrix products, arithmetic and copies ran while one was open for 3% of the time, Pallas kernels for 0%

commit v1 on v0

--- a/solution.py
+++ b/solution.py
@@ -70,7 +70,7 @@
         yright = jnp.take(disp, rrow, axis=0)
         nextone = passed_along(yleft, "sub", -1)
         image = (cut * (yright - nextone))[None]
-        alpha = rz_now / lax.psum(local_dot(direc, image), ("sub", "grp"))
+        alpha = rz_now / lax.psum(lax.psum(local_dot(direc, image), "sub"), "grp")
         multipliers = multipliers + alpha * direc
         residual = residual - alpha * image
         if step + 1 < ITERS:

time: 929 us -> 1180 us (1.27)
  blocking collectives: 518 us -> 777 us
    psum x2 -> x6, blocking collectives: 214 us -> 480 us  [local(): alpha = rz_now / lax.psum(lax.psum(local_dot(direc, image), 'sub'), 'grp')]
where the time goes in v1:
time: 1180 us
  blocking collectives  777 us (66%)
  waiting for transfers between devices  212 us (18%)
  matrix products  66.8 us (6%)
  other arithmetic  53 us (4%)
  starting transfers between devices  32.4 us (3%)
  local copies, waits for them, and re-layouts  22.8 us (2%)
  between operations  14.6 us (1%)
    psum x6, blocking collectives, local(): alpha = rz_now / lax.psum(lax.psum(local_dot(direc, image), 'sub'), 'grp')  480 us
    psum x3, blocking collectives, norm_total(): return lax.psum(value, ('sub', 'grp'))  297 us
    psum x3, waiting for transfers between devices, local(): summed = lax.psum(primal, 'grp')  188 us
    ppermute x6, starting transfers between devices, passed_along(): lax.ppermute(shard, axis, [(i, (i + by) % peers) for i in range(peers)])  31.9 us
    scatter-add x6, other arithmetic, local(): interior_load = zeros.at[rrow].add(apply_own).at[lrow].add(-apply_left)  24.6 us
  transfers between devices with their start and end apart: 9, of which 8 were waited for; matrix products, arithmetic and copies ran while one was open for 3% of the time, Pallas kernels for 0%

profile of v1, /device:TPU:1, one launch (start us, length us, event | category | flops | bytes accessed | tf_op | source)
XLA Modules:
  0.0 1178.2 jit_solution(6703106193194130141)
XLA Ops:
  9.1 4.4 collective-permute-start
  16.2 3.6 scatter_custom_fusion
  20.4 8.8 collective-permute-done
  29.9 4.7 scatter_custom_fusion.1
  34.7 2.5 fusion.46
  46.2 2.7 convolution_bitcast_fusion.14
  49.2 2.7 convolution_bitcast_fusion.9
  51.8 67.6 %all-reduce.4.cloned.1.call-done = f32[128,256]{0,1:T(8,128)} async-done(((f32[128,256]{0,1:T(8,128)}), f32[128,256]{0,1:T(8,128)}) %all-reduce.4.cloned.1.call-update) | async-done | bytes 131088 | tf_op jit(solution)/shard_map/psum | solution.py:52
  120.6 3.3 fusion.2
  123.9 2.7 copy.17
  126.6 2.9 gather_fusion.1
  131.3 7.0 collective-permute-start.1
  139.7 2.9 gather_fusion
  144.5 115.3 %psum.86 = f32[256]{0:T(256)} all-reduce(f32[256]{0:T(256)S(1)} %get-tuple-element.3), channel_id=1, replica_groups=mesh['sub'=64,'grp'=8] {'sub'}, use_global_device_ids=true, to_apply=%region_6.8 | all-reduce | flops 256 | bytes 2048 | tf_op jit(solution)/shard_map/psum | solution.py:73
  259.8 44.5 %psum.87 = f32[256]{0:T(256)} all-reduce(f32[256]{0:T(256)} %psum.86), channel_id=1, replica_groups=mesh['sub'=64,'grp'=8] {'grp'}, use_global_device_ids=true, to_apply=%region_7.9 | all-reduce | flops 256 | bytes 2048 | tf_op jit(solution)/shard_map/psum | solution.py:73
  304.4 98.7 %psum.84 = f32[256]{0:T(256)S(1)} all-reduce(f32[256]{0:T(256)} %get-tuple-element.4), channel_id=1, replica_groups=mesh['sub'=64,'grp'=8] {'sub','grp'}, use_global_device_ids=true, to_apply=%region_1.0 | all-reduce | flops 256 | bytes 2048 | tf_op jit(solution)/shard_map/psum | solution.py:16
  403.8 2.6 fusion.87
  406.3 99.6 %psum.88 = f32[256]{0:T(256)S(1)} all-reduce(f32[256]{0:T(256)} %get-tuple-element.7), channel_id=1, replica_groups=mesh['sub'=64,'grp'=8] {'sub','grp'}, use_global_device_ids=true, to_apply=%region_9.11 | all-reduce | flops 256 | bytes 2048 | tf_op jit(solution)/shard_map/psum | solution.py:16
  508.4 2.7 collective-permute-start.2
  511.2 3.4 scatter_custom_fusion.2
  514.6 6.6 collective-permute-done.2
  521.1 4.9 scatter_custom_fusion.3
  526.0 3.3 fusion.43
  529.3 2.7 convolution_bitcast_fusion.13
  543.1 2.6 convolution_bitcast_fusion.6
  545.7 61.3 %all-reduce.6.cloned.1.call-done = f32[128,256]{0,1:T(8,128)} async-done(((f32[128,256]{0,1:T(8,128)}), f32[128,256]{0,1:T(8,128)}) %all-reduce.6.cloned.1.call-update) | async-done | bytes 131088 | tf_op jit(solution)/shard_map/psum | solution.py:52
  608.2 3.4 fusion.1
  611.6 2.6 copy.19
  614.2 3.0 gather_fusion.3
  619.0 7.0 collective-permute-start.3
  626.0 3.1 gather_fusion.2
  631.5 116.0 %psum.90 = f32[256]{0:T(256)} all-reduce(f32[256]{0:T(256)} %multiply_reduce_fusion.1), channel_id=1, replica_groups=mesh['sub'=64,'grp'=8] {'sub'}, use_global_device_ids=true, to_apply=%region_14.16 | all-reduce | flops 256 | bytes 2048 | tf_op jit(solution)/shard_map/psum | solution.py:73
  747.5 44.5 %psum.91 = f32[256]{0:T(256)} all-reduce(f32[256]{0:T(256)} %psum.90), channel_id=1, replica_groups=mesh['sub'=64,'grp'=8] {'grp'}, use_global_device_ids=true, to_apply=%region_15.17 | all-reduce | flops 256 | bytes 2048 | tf_op jit(solution)/shard_map/psum | solution.py:73
  793.3 2.6 fusion.88
  795.9 98.7 %psum.92 = f32[256]{0:T(256)} all-reduce(f32[256]{0:T(256)} %get-tuple-element.5), channel_id=1, replica_groups=mesh['sub'=64,'grp'=8] {'sub','grp'}, use_global_device_ids=true, to_apply=%region_17.19 | all-reduce | flops 256 | bytes 2048 | tf_op jit(solution)/shard_map/psum | solution.py:16
  897.1 3.7 collective-permute-start.4
  900.7 3.4 scatter_custom_fusion.4
  904.1 5.4 collective-permute-done.4
  909.5 4.7 scatter_custom_fusion.5
  914.2 3.3 fusion.40
  917.5 2.7 convolution_bitcast_fusion.12
  931.0 3.0 convolution_bitcast_fusion.3
  934.0 59.5 %all-reduce.8.cloned.1.call-done = f32[128,256]{0,1:T(8,128)} async-done(((f32[128,256]{0,1:T(8,128)}), f32[128,256]{0,1:T(8,128)}) %all-reduce.8.cloned.1.call-update) | async-done | bytes 131088 | tf_op jit(solution)/shard_map/psum | solution.py:52
  994.6 2.2 fusion
  998.5 7.1 collective-permute-start.5
  1006.8 2.2 collective-permute-done.5
  1010.1 115.5 %psum.94 = f32[256]{0:T(256)S(1)} all-reduce(f32[256]{0:T(256)S(1)} %multiply_reduce_fusion), channel_id=1, replica_groups=mesh['sub'=64,'grp'=8] {'sub'}, use_global_device_ids=true, to_apply=%region_22.24 | all-reduce | flops 256 | bytes 2048 | tf_op jit(solution)/shard_map/psum | solution.py:73
  1125.5 43.8 %psum.95 = f32[256]{0:T(256)S(1)} all-reduce(f32[256]{0:T(256)S(1)} %psum.94), channel_id=1, replica_groups=mesh['sub'=64,'grp'=8] {'grp'}, use_global_device_ids=true, to_apply=%region_23.25 | all-reduce | flops 256 | bytes 2048 | tf_op jit(solution)/shard_map/psum | solution.py:73
  (132 shorter events, 62.2 us)
Async XLA Ops:
  7.2 39.0 %copy-start = (f32[1,1,3,384,128]{4,3,2,1,0:T(8,128)S(1)}, f32[1,1,3,384,128]{4,3,2,1,0:T(8,128)}, u32[]{:S(2)}) copy-start(f32[1,1,3,384,128]{4,3,2,1,0:T(8,128)} %param.18) | copy-start | bytes 1769476
  7.2 12.7 %copy-start.32 = (s32[1,1,256]{2,1,0:T(1,128)S(1)}, s32[1,1,256]{2,1,0:T(1,128)}, u32[]{:S(2)}) copy-start(s32[1,1,256]{2,1,0:T(1,128)} %param.15) | copy-start | bytes 3076
  7.2 112.2 %all-reduce.4.cloned.1.call-start = ((), (), s32[]{:S(2)}) async-start(), calls=%async_computation | async-start | bytes 262144 | tf_op jit(solution)/shard_map/psum | solution.py:52
  9.1 20.1 %collective-permute-start = (f32[256,256]{1,0:T(8,128)S(1)}, f32[256,256]{1,0:T(8,128)S(1)}, u32[]{:S(2)}, u32[]{:S(2)}) collective-permute-start(f32[256,256]{1,0:T(8,128)S(1)} %fusion.98), channel_id=1, source_target_pairs={{0,8},{8,16},{16,24},{24,32},{32,40},{40,48},{48,56},{56,64},{64,7... | collective-permute-start | bytes 786440 | tf_op jit(solution)/shard_map/ppermute | solution.py:12
  14.1 20.5 %copy-start.33 = (s32[256,1]{0,1:T(1,128)}, s32[256,1]{0,1:T(1,128)S(1)}, u32[]{:S(2)}) copy-start(s32[256,1]{0,1:T(1,128)S(1)} %compare_select_fusion) | copy-start | bytes 3076
  15.5 114.1 %copy-start.30 = (pred[256]{0:T(512)(128)(4,1)}, pred[256]{0:T(512)(128)(4,1)S(1)}, u32[]{:S(2)}) copy-start(pred[256]{0:T(512)(128)(4,1)S(1)} %compare_and_fusion) | copy-start | bytes 772
  16.2 13.0 %copy-start.34 = (s32[256,1]{0,1:T(1,128)}, s32[256,1]{0,1:T(1,128)S(1)}, u32[]{:S(2)}) copy-start(s32[256,1]{0,1:T(1,128)S(1)} %compare_select_fusion.1) | copy-start | bytes 3076
  16.2 110.4 %copy-start.22 = (s32[1024]{0:T(1024)}, s32[1024]{0:T(1024)S(1)}, u32[]{:S(2)}) copy-start(s32[1024]{0:T(1024)S(1)} %pad_clamp_fusion) | copy-start | bytes 12292
  16.2 18.4 %copy-start.1 = (f32[1,1,3,384,384]{4,3,2,1,0:T(8,128)S(1)}, f32[1,1,3,384,384]{4,3,2,1,0:T(8,128)}, u32[]{:S(2)}) copy-start(f32[1,1,3,384,384]{4,3,2,1,0:T(8,128)} %param.16) | copy-start | bytes 5308420
  29.2 0.7 copy-start.20
  29.9 7.3 copy-start.2
  34.6 3.4 copy-start.7
  42.7 1.8 copy-start.9
  44.5 1.7 copy-start.10
  48.9 558.1 %all-reduce.6.cloned.1.call-start = ((), (), s32[]{:S(2)}) async-start(), calls=%async_computation.1 | async-start | bytes 262144 | tf_op jit(solution)/shard_map/psum | solution.py:52
  131.3 11.3 collective-permute-start.1
  139.0 3.6 copy-start.23
  139.7 3.0 copy-start.21
  403.1 3.2 copy-start.25
  403.8 2.6 copy-start.26
  508.4 12.7 %collective-permute-start.2 = (f32[256,256]{1,0:T(8,128)}, f32[256,256]{1,0:T(8,128)}, u32[]{:S(2)}, u32[]{:S(2)}) collective-permute-start(f32[256,256]{1,0:T(8,128)} %multiply_add_fusion.1), channel_id=1, source_target_pairs={{0,8},{8,16},{16,24},{24,32},{32,40},{40,48},{48,56},{56,64},{64,7... | collective-permute-start | bytes 786440 | tf_op jit(solution)/shard_map/ppermute | solution.py:12
  526.0 3.3 copy-start.5
  532.0 1.9 copy-start.6
  538.5 1.8 copy-start.11
  538.6 2.6 copy-start.16
  540.4 0.7 copy-start.14
  542.8 450.6 %all-reduce.8.cloned.1.call-start = ((), (), s32[]{:S(2)}) async-start(), calls=%async_computation.2 | async-start | bytes 262144 | tf_op jit(solution)/shard_map/psum | solution.py:52
  619.0 10.6 collective-permute-start.3
  792.7 0.6 copy-start.28
  897.1 12.4 %collective-permute-start.4 = (f32[256,256]{1,0:T(8,128)}, f32[256,256]{1,0:T(8,128)}, u32[]{:S(2)}, u32[]{:S(2)}) collective-permute-start(f32[256,256]{1,0:T(8,128)} %multiply_add_fusion), channel_id=1, source_target_pairs={{0,8},{8,16},{16,24},{24,32},{32,40},{40,48},{48,56},{56,64},{64,7... | collective-permute-start | bytes 786440 | tf_op jit(solution)/shard_map/ppermute | solution.py:12
  914.2 3.3 copy-start.3
  920.2 1.9 copy-start.4
  926.7 1.8 copy-start.12
  926.7 2.6 copy-start.17
  928.6 0.7 copy-start.15
  931.0 62.5 %copy-start.19 = (f32[1,128,128]{2,1,0:T(8,128)S(1)}, f32[1,128,128]{2,1,0:T(8,128)}, u32[]{:S(2)}) copy-start(f32[1,128,128]{2,1,0:T(8,128)} %param.19) | copy-start | bytes 196612
  931.0 63.6 %copy-start.13 = (f32[256,384]{1,0:T(8,128)S(1)}, f32[256,384]{1,0:T(8,128)}, u32[]{:S(2)}) copy-start(f32[256,384]{1,0:T(8,128)} %copy-done.12) | copy-start | bytes 1179652
  997.2 1.1 copy-start.31
  998.5 170.9 %copy-start.24 = (f32[256]{0:T(256)S(1)}, f32[256]{0:T(256)}, u32[]{:S(2)}) copy-start(f32[256]{0:T(256)} %psum.92) | copy-start | bytes 3076
  998.5 170.9 %copy-start.8 = (f32[1,1,256,256]{3,2,1,0:T(8,128)S(1)}, f32[1,1,256,256]{3,2,1,0:T(8,128)}, u32[]{:S(2)}) copy-start(f32[1,1,256,256]{3,2,1,0:T(8,128)} %param.11) | copy-start | bytes 786436
  998.5 170.9 %copy-start.18 = (f32[256,256]{1,0:T(8,128)S(1)}, f32[256,256]{1,0:T(8,128)}, u32[]{:S(2)}) copy-start(f32[256,256]{1,0:T(8,128)} %get-tuple-element.6) | copy-start | bytes 786436
  998.5 170.9 %copy-start.27 = (f32[256]{0:T(256)S(1)}, f32[256]{0:T(256)}, u32[]{:S(2)}) copy-start(f32[256]{0:T(256)} %copy-done.26) | copy-start | bytes 3076
  998.5 170.9 %copy-start.29 = (f32[256]{0:T(256)S(1)}, f32[256]{0:T(256)}, u32[]{:S(2)}) copy-start(f32[256]{0:T(256)} %copy-done.28) | copy-start | bytes 3076
  998.5 10.4 collective-permute-start.5
Sparse Core Ops, SparseCore 0:
  49.0 70.3 all-reduce.3
  543.0 63.9 all-reduce.5
  931.1 62.2 all-reduce.7
